TPU v7x, 32 devices: a whole 2x2x4 slice. The times are simulated.
32 devices in a mesh: dp: 16 (over z, x, core), mp: 2 (over y).
Axes of the slice: x: 2, y: 2, z: 4, core: 2. Of those that a mesh axis runs over, the one named last changes fastest.
Arguments:
- features: bfloat16 [2048, 512], P('dp'), may hold values from -6 to 6
- w_in: bfloat16 [512, 512], P(None, 'mp'), may hold values from -0.25 to 0.25
- b_in: float32 [512], P('mp'), may hold values from -1 to 1
- w_out: bfloat16 [512, 128], P('mp'), may hold values from -0.25 to 0.25
- partner: int32 [2048], P('dp'), may hold values from 0 to 2047, as said below
- window: int32 [16], replicated, may hold values from 0 to 3
Outputs:
- row_loss: float32 [512], P('dp')
- grad_w_in: float32 [512, 512], P(None, 'mp')
- grad_b_in: float32 [512], P('mp')
- grad_w_out: float32 [512, 128], P('mp')
Inputs may be any that keep to these rules, and one draw needn't show every extreme that they name: partner pairs the rows: partner[partner[i]] = i and partner[i] != i for every row i.
All inputs are finite; a program needn't handle non-finite values.
Results may differ from a plain program's by a relative error of at most 0.0027.
Values may be sent and summed in bfloat16 or wider, within the bound.
A program may use at most 64 MiB of HBM per device.

v0:
```python
import math
import jax
import jax.numpy as jnp
from jax import lax
from jax.sharding import PartitionSpec as P

A_DEV = 32
INV_TEMP = 10.0
SHIFT = 10.0
EPS = 1e-06


def contract_rows(left, right):
    return lax.dot_general(
        left, right, (((0,), (0,)), ((), ())), preferred_element_type=jnp.float32
    )


def on_device(features, w_in, b_in, w_out, partner, window):
    rows = features.shape[0]
    parts = lax.axis_size("mp")
    part = lax.axis_index("mp")
    shards = lax.axis_size("dp")
    shard = lax.axis_index("dp")
    width = rows // parts
    anchor_rows = A_DEV
    anchor_all = anchor_rows * shards
    pre = jnp.dot(features, w_in, preferred_element_type=jnp.float32) + b_in
    hidden = jax.nn.silu(pre).astype(jnp.bfloat16)
    proj = lax.psum(jnp.dot(hidden, w_out, preferred_element_type=jnp.float32), "mp")
    norm = jnp.sqrt(jnp.sum(proj * proj, axis=1, keepdims=True) + EPS)
    emb = (proj / norm).astype(jnp.bfloat16)
    embed = emb.shape[1]
    own_cols = lax.dynamic_slice_in_dim(emb, part * width, width, 0)
    columns = lax.all_gather(own_cols, "dp", axis=0, tiled=True)
    col_total = columns.shape[0]
    shard_ids = jnp.arange(shards, dtype=jnp.int32)
    my_block = jnp.sum(jnp.where(shard_ids == shard, window, 0))
    my_start = my_block * anchor_rows
    anchors = lax.dynamic_slice_in_dim(emb, my_start, anchor_rows, 0)
    anchor_partner = lax.dynamic_slice_in_dim(partner, my_start, anchor_rows, 0)
    anchor_ids = shard * rows + my_start + jnp.arange(anchor_rows, dtype=jnp.int32)

    def column_ids(start, count):
        local = start + jnp.arange(count, dtype=jnp.int32)
        return local // width * rows + part * width + local % width

    blk = math.gcd(col_total, 2048)
    nblk = col_total // blk
    col_blocks = columns.reshape(nblk, blk, embed)
    starts = jnp.arange(nblk, dtype=jnp.int32) * blk

    def forward(carry, item):
        total, hit = carry
        block, start = item
        s = jnp.dot(anchors, block.T, preferred_element_type=jnp.float32) * INV_TEMP
        ids = column_ids(start, blk)
        ex = jnp.where(ids[None, :] == anchor_ids[:, None], 0.0, jnp.exp(s - SHIFT))
        hit = hit + jnp.sum(jnp.where(ids[None, :] == anchor_partner[:, None], s, 0.0), axis=1)
        return ((total + jnp.sum(ex, axis=1), hit), None)

    zero_rows = jnp.zeros((anchor_rows,), jnp.float32)
    (total, hit), _ = lax.scan(forward, (zero_rows, zero_rows), (col_blocks, starts))
    total, hit = lax.psum((total, hit), "mp")
    row_loss = jnp.log(total) + SHIFT - hit

    def row_weights(s, ids):
        prob = jnp.where(
            ids[None, :] == anchor_ids[:, None], 0.0, jnp.exp(s - SHIFT) / total[:, None]
        )
        onehot = (ids[None, :] == anchor_partner[:, None]).astype(jnp.float32)
        return (prob - onehot).astype(jnp.bfloat16)

    def backward(acc, item):
        block, start = item
        s = jnp.dot(anchors, block.T, preferred_element_type=jnp.float32) * INV_TEMP
        weights = row_weights(s, column_ids(start, blk))
        return (acc + jnp.dot(weights, block, preferred_element_type=jnp.float32), None)

    row_part, _ = lax.scan(
        backward, jnp.zeros((anchor_rows, embed), jnp.float32), (col_blocks, starts)
    )
    totals = lax.all_gather(total, "dp", axis=0, tiled=True)
    own_ids = shard * rows + part * width + jnp.arange(width, dtype=jnp.int32)
    own_partner = lax.dynamic_slice_in_dim(partner, part * width, width, 0)
    piece = lax.all_gather(anchors, "dp", axis=0, tiled=True)
    count = piece.shape[0]
    inner = math.gcd(count, 2048)
    sub_pieces = piece.reshape(count // inner, inner, embed)
    offsets = jnp.arange(count // inner, dtype=jnp.int32) * inner

    def one_block(inner_acc, item):
        block, offset = item
        block_totals = lax.dynamic_slice_in_dim(totals, offset, inner, 0)
        flat = offset + jnp.arange(inner, dtype=jnp.int32)
        owner = flat // anchor_rows
        owner_block = jnp.sum(
            jnp.where(owner[:, None] == shard_ids[None, :], window[None, :], 0), axis=1
        )
        ids = owner * rows + owner_block * anchor_rows + flat % anchor_rows
        s = jnp.dot(own_cols, block.T, preferred_element_type=jnp.float32) * INV_TEMP
        prob = jnp.where(
            ids[None, :] == own_ids[:, None], 0.0, jnp.exp(s - SHIFT) / block_totals[None, :]
        )
        onehot = (ids[None, :] == own_partner[:, None]).astype(jnp.float32)
        weights = (prob - onehot).astype(jnp.bfloat16)
        return (inner_acc + jnp.dot(weights, block, preferred_element_type=jnp.float32), None)

    result, _ = lax.scan(one_block, jnp.zeros((width, embed), jnp.float32), (sub_pieces, offsets))
    placed = lax.dynamic_update_slice_in_dim(
        jnp.zeros((rows, embed), jnp.float32), result, part * width, 0
    )
    row_placed = lax.dynamic_update_slice_in_dim(
        jnp.zeros((rows, embed), jnp.float32), row_part, my_start, 0
    )
    grad_emb = lax.psum(row_placed + placed, "mp") * (INV_TEMP / anchor_all)
    unit = proj / norm
    grad_proj = ((grad_emb - unit * jnp.sum(unit * grad_emb, axis=1, keepdims=True)) / norm).astype(
        jnp.bfloat16
    )
    grad_w_out = contract_rows(hidden, grad_proj)
    grad_hidden = lax.dot_general(
        grad_proj, w_out, (((1,), (1,)), ((), ())), preferred_element_type=jnp.float32
    )
    sig = jax.nn.sigmoid(pre)
    grad_pre = (grad_hidden * sig * (1.0 + pre * (1.0 - sig))).astype(jnp.bfloat16)
    grad_w_in = contract_rows(features, grad_pre)
    grad_b_in = jnp.sum(grad_pre.astype(jnp.float32), axis=0)
    grad_w_in, grad_b_in, grad_w_out = lax.psum((grad_w_in, grad_b_in, grad_w_out), "dp")
    return (row_loss, grad_w_in, grad_b_in, grad_w_out)


def solution(mesh):
    return jax.shard_map(
        on_device,
        mesh=mesh,
        in_specs=(P("dp", None), P(None, "mp"), P("mp"), P("mp", None), P("dp"), P()),
        out_specs=(P("dp"), P(None, "mp"), P("mp"), P("mp", None)),
        check_vma=False,
    )
```

profile of v0, /device:TPU:0, one launch (start us, length us, event | category | flops | bytes accessed | tf_op | source)
XLA Modules:
  0.0 234.8 jit_solution(11536599049466594532)
XLA Ops:
  7.2 0.0 copy-start
  7.2 0.0 copy-start.6
  7.2 0.0 all-reduce.7.cloned.1.call-start
  7.2 0.9 copy-done
  8.1 1.1 multiply_convert_fusion
  9.2 0.0 copy-done.6
  9.3 0.8 fusion.57
  10.0 0.0 all-reduce.7.cloned.1.call-update
  10.1 0.0 all-reduce.9.cloned.1.call-start
  10.1 0.0 copy-start.7
  10.1 0.6 copy-done.7
  10.8 0.6 fusion.50
  12.1 0.0 copy-start.8
  12.1 0.6 copy-done.8
  12.8 0.1 dynamic_slice.31
  12.8 0.1 dynamic_slice.32
  12.9 0.1 select_reduce_fusion
  13.0 0.6 copy-done.9
  13.7 0.6 dynamic-slice.3
  14.9 19.6 %all-reduce.7.cloned.1.call-done = f32[128,128]{1,0:T(8,128)} async-done(((f32[128,128]{1,0:T(8,128)}), f32[128,128]{1,0:T(8,128)}) %all-reduce.7.cloned.1.call-update) | async-done | bytes 65552 | tf_op jit(solution)/shard_map/psum | solution.py:30
  34.5 1.0 multiply_reduce_fusion.1
  35.6 0.1 fusion.56
  35.7 21.7 %all_gather.10 = bf16[512,128]{1,0:T(8,128)(2,1)S(1)} all-gather(bf16[32,128]{1,0:T(8,128)(2,1)S(1)} %constant_dynamic-slice_fusion.1), channel_id=1, replica_groups=mesh['dp'=16,'mp'=2] {'dp'}, dimensions={0}, use_global_device_ids=true | all-gather | bytes 139264 | tf_op jit(solution)/shard_map/all_gather | solution.py:86
  57.4 18.1 %all_gather.9 = bf16[1024,128]{1,0:T(8,128)(2,1)S(1)} all-gather(bf16[64,128]{1,0:T(8,128)(2,1)S(1)} %constant_dynamic-slice_fusion), channel_id=1, replica_groups=mesh['dp'=16,'mp'=2] {'dp'}, dimensions={0}, use_global_device_ids=true | all-gather | bytes 278528 | tf_op jit(solution)/shard_map/all_gather | solution.py:35
  75.5 0.3 fusion.11
  75.8 4.9 %all-reduce.2 = (f32[32]{0:T(128)S(1)}, f32[32]{0:T(128)S(1)}) all-reduce(f32[32]{0:T(128)S(1)} %get-tuple-element.70, f32[32]{0:T(128)S(1)} %get-tuple-element.69), channel_id=1, replica_groups=mesh['dp'=16,'mp'=2] {'mp'}, use_global_device_ids=true, to_apply=%region_6.7 | all-reduce | flops 64 | bytes 512 | tf_op jit(solution)/shard_map/psum | solution.py:64
  80.8 0.2 dynamic-update-slice.1
  81.0 29.9 %all-reduce = f32[512]{0:T(512)S(1)} all-reduce(f32[512]{0:T(512)S(1)} %dynamic-update-slice.1), channel_id=1, replica_groups=mesh['dp'=16,'mp'=2] {'dp'}, use_global_device_ids=true, to_apply=%add | all-reduce | flops 512 | bytes 4096
  110.9 0.2 convolution_dynamic-update-slice_fusion
  111.1 0.3 fusion.10
  111.4 0.0 copy-start.3
  111.5 0.6 copy-done.3
  112.1 0.0 all-reduce.9.cloned.1.call-update
  112.1 0.0 all-reduce.11.cloned.1.call-start
  112.2 17.4 %all-reduce.9.cloned.1.call-done = f32[128,128]{1,0:T(8,128)} async-done(((f32[128,128]{1,0:T(8,128)}), f32[128,128]{1,0:T(8,128)}) %all-reduce.9.cloned.1.call-update) | async-done | bytes 65552 | tf_op jit(solution)/shard_map/psum | solution.py:116
  129.6 1.1 multiply_reduce_fusion
  130.6 0.0 copy-done.2
  130.7 0.1 divide_convert_fusion
  130.8 0.9 fusion.58
  131.6 0.2 convert_reduce_fusion
  131.8 0.7 copy-done.5
  132.5 1.0 convolution_bitcast_fusion
  133.6 0.0 all-reduce.11.cloned.1.call-update
  133.6 0.5 add_subtract_fusion
  134.1 33.6 %psum.54 = f32[256]{0:T(256)} all-reduce(f32[256]{0:T(256)S(1)} %get-tuple-element.87), channel_id=1, replica_groups=mesh['dp'=16,'mp'=2] {'dp'}, use_global_device_ids=true, to_apply=%region_12.13 | all-reduce | flops 256 | bytes 2048 | tf_op jit(solution)/shard_map/psum | solution.py:129
  167.7 57.9 %all-reduce.11.cloned.1.call-done = (f32[512,256]{0,1:T(8,128)}, f32[256,128]{1,0:T(8,128)}) async-done(((f32[512,256]{0,1:T(8,128)}, f32[256,128]{1,0:T(8,128)}), (f32[512,256]{0,1:T(8,128)}, f32[256,128]{1,0:T(8,128)})) %all-reduce.11.cloned.1.call-update) | async-done | bytes 655376 | tf_op jit(solution)/shard_map/psum | solution.py:129
  225.5 2.1 copy.11
  227.6 0.7 copy.19
  (17 shorter events, 0.1 us)
Async XLA Ops:
  7.2 1.0 copy-start
  7.2 2.1 copy-start.6
  7.2 27.3 %all-reduce.7.cloned.1.call-start = ((), (), s32[]{:S(2)}) async-start(), calls=%async_computation | async-start | bytes 131072 | tf_op jit(solution)/shard_map/psum | solution.py:30
  10.1 119.5 %all-reduce.9.cloned.1.call-start = ((), (), s32[]{:S(2)}) async-start(), calls=%async_computation.1 | async-start | bytes 131072 | tf_op jit(solution)/shard_map/psum | solution.py:116
  10.1 0.7 copy-start.7
  12.1 0.7 copy-start.8
  13.0 0.7 copy-start.9
  34.5 1.0 copy-start.1
  111.4 0.6 copy-start.3
  112.1 113.4 %all-reduce.11.cloned.1.call-start = ((), (), s32[]{:S(2)}) async-start(), calls=%async_computation.2 | async-start | bytes 1310720 | tf_op jit(solution)/shard_map/psum | solution.py:129
  129.6 1.1 copy-start.2
  131.6 0.9 copy-start.5
  225.5 2.1 copy-start.4
Sparse Core Ops, SparseCore 0:
  10.8 23.6 all-reduce.6
  112.2 17.2 all-reduce.8
  133.7 91.7 all-reduce.10
where the time goes:
time: 235 us
  blocking collectives  108 us (46%)
  waiting for transfers between devices  94.9 us (40%)
  between operations  15.3 us (7%)
  local copies, waits for them, and re-layouts  7.86 us (3%)
  matrix products  4.84 us (2%)
  other arithmetic  3.56 us (2%)
    psum x1, waiting for transfers between devices, on_device(): lax.psum((grad_w_in, grad_b_in, grad_w_out), 'dp')  57.9 us
    psum x1, blocking collectives, on_device(): lax.psum((grad_w_in, grad_b_in, grad_w_out), 'dp')  33.6 us
    unnamed x1, blocking collectives  29.9 us
    all_gather x1, blocking collectives, on_device(): piece = lax.all_gather(anchors, 'dp', axis=0, tiled=True)  21.7 us
    psum x1, waiting for transfers between devices, on_device(): lax.psum(jnp.dot(hidden, w_out, preferred_element_type=jnp.float32), 'mp')  19.6 us
    all_gather x1, blocking collectives, on_device(): columns = lax.all_gather(own_cols, 'dp', axis=0, tiled=True)  18.1 us
    psum x1, waiting for transfers between devices, on_device(): grad_emb = lax.psum(row_placed + placed, 'mp') * (INV_TEMP / anchor_all)  17.4 us
    unnamed x25, local copies, waits for them, and re-layouts  7.68 us
  transfers between devices with their start and end apart: 3, of which 3 were waited for; matrix products, arithmetic and copies ran while one was open for 1% of the time, Pallas kernels for 0%

commit v1 on v0

--- a/solution.py
+++ b/solution.py
@@ -32,7 +32,14 @@
     emb = (proj / norm).astype(jnp.bfloat16)
     embed = emb.shape[1]
     own_cols = lax.dynamic_slice_in_dim(emb, part * width, width, 0)
-    columns = lax.all_gather(own_cols, "dp", axis=0, tiled=True)
+    size = lax.axis_size("dp")
+    forward_2 = [(i, (i + 1) % size) for i in range(size)]
+    pieces = [own_cols]
+    for far in range(1, size):
+        pieces = [lax.ppermute(pieces[0], "dp", forward_2), *pieces]
+    full = jnp.concatenate(pieces, axis=0)
+    shift = (lax.axis_index("dp") + 1) * pieces[-1].shape[0]
+    columns = jnp.roll(full, shift, axis=0)
     col_total = columns.shape[0]
     shard_ids = jnp.arange(shards, dtype=jnp.int32)
     my_block = jnp.sum(jnp.where(shard_ids == shard, window, 0))

time: 235 us -> 295 us (1.26)
  waiting for transfers between devices: 94.9 us -> 177 us
  blocking collectives: 108 us -> 86.3 us
    ppermute x0 -> x15, waiting for transfers between devices: none -> 77.9 us  [on_device(): pieces = [lax.ppermute(pieces[0], 'dp', forward_2), *pieces]]
    all_gather x1 -> x0, blocking collectives: 18.1 us -> none  [on_device(): columns = lax.all_gather(own_cols, 'dp', axis=0, tiled=True)]
    psum x1, waiting for transfers between devices: 19.6 us -> 24.4 us  [on_device(): lax.psum(jnp.dot(hidden, w_out, preferred_element_type=jnp.float32), 'mp')]
    all_gather x1, blocking collectives: 21.7 us -> 18.3 us  [on_device(): piece = lax.all_gather(anchors, 'dp', axis=0, tiled=True)]
    unnamed x25 -> x56, local copies, waits for them, and re-layouts: 7.68 us -> 7.35 us
  transfers between devices with their start and end apart: 3 -> 18, of which waited for: 3 -> 17; matrix products, arithmetic and copies ran while one was open for 1% -> 1% of each run, Pallas kernels for 0% -> 0%
where the time goes in v1:
time: 295 us
  waiting for transfers between devices  177 us (60%)
  blocking collectives  86.3 us (29%)
  between operations  15.3 us (5%)
  local copies, waits for them, and re-layouts  7.53 us (3%)
  matrix products  4.86 us (2%)
  other arithmetic  3.56 us (1%)
    ppermute x15, waiting for transfers between devices, on_device(): pieces = [lax.ppermute(pieces[0], 'dp', forward_2), *pieces]  77.9 us
    psum x1, waiting for transfers between devices, on_device(): lax.psum((grad_w_in, grad_b_in, grad_w_out), 'dp')  57.8 us
    psum x1, blocking collectives, on_device(): lax.psum((grad_w_in, grad_b_in, grad_w_out), 'dp')  33.6 us
    unnamed x1, blocking collectives  29.5 us
    psum x1, waiting for transfers between devices, on_device(): lax.psum(jnp.dot(hidden, w_out, preferred_element_type=jnp.float32), 'mp')  24.4 us
    all_gather x1, blocking collectives, on_device(): piece = lax.all_gather(anchors, 'dp', axis=0, tiled=True)  18.3 us
    psum x1, waiting for transfers between devices, on_device(): grad_emb = lax.psum(row_placed + placed, 'mp') * (INV_TEMP / anchor_all)  17.1 us
    unnamed x56, local copies, waits for them, and re-layouts  7.35 us
  transfers between devices with their start and end apart: 18, of which 17 were waited for; matrix products, arithmetic and copies ran while one was open for 1% of the time, Pallas kernels for 0%

profile of v1, /device:TPU:0, one launch (start us, length us, event | category | flops | bytes accessed | tf_op | source)
XLA Modules:
  0.0 295.1 jit_solution(12894953340705878339)
XLA Ops:
  7.2 0.9 copy-done
  8.1 1.1 multiply_convert_fusion
  9.3 0.8 fusion.61
  10.1 24.4 %all-reduce.7.cloned.1.call-done = f32[128,128]{1,0:T(8,128)} async-done(((f32[128,128]{1,0:T(8,128)}), f32[128,128]{1,0:T(8,128)}) %all-reduce.7.cloned.1.call-update) | async-done | bytes 65552 | tf_op jit(solution)/shard_map/psum | solution.py:30
  34.5 1.0 multiply_reduce_fusion.1
  35.6 0.1 fusion.60
  35.7 0.1 collective-permute-start
  35.8 5.8 %collective-permute-done = bf16[64,128]{1,0:T(8,128)(2,1)S(1)} collective-permute-done((bf16[64,128]{1,0:T(8,128)(2,1)S(1)}, bf16[64,128]{1,0:T(8,128)(2,1)S(1)}, u32[]{:S(2)}, u32[]{:S(2)}) %collective-permute-start) | collective-permute-done | bytes 16416 | tf_op jit(solution)/shard_map/ppermute | solution.py:39
  41.6 5.9 %collective-permute-done.1 = bf16[64,128]{1,0:T(8,128)(2,1)S(1)} collective-permute-done((bf16[64,128]{1,0:T(8,128)(2,1)S(1)}, bf16[64,128]{1,0:T(8,128)(2,1)S(1)}, u32[]{:S(2)}, u32[]{:S(2)}) %collective-permute-start.1) | collective-permute-done | bytes 16416 | tf_op jit(solution)/shard_map/ppermute | solution.py:39
  47.5 5.9 %collective-permute-done.2 = bf16[64,128]{1,0:T(8,128)(2,1)S(1)} collective-permute-done((bf16[64,128]{1,0:T(8,128)(2,1)S(1)}, bf16[64,128]{1,0:T(8,128)(2,1)S(1)}, u32[]{:S(2)}, u32[]{:S(2)}) %collective-permute-start.2) | collective-permute-done | bytes 16416 | tf_op jit(solution)/shard_map/ppermute | solution.py:39
  53.3 5.9 %collective-permute-done.3 = bf16[64,128]{1,0:T(8,128)(2,1)S(1)} collective-permute-done((bf16[64,128]{1,0:T(8,128)(2,1)S(1)}, bf16[64,128]{1,0:T(8,128)(2,1)S(1)}, u32[]{:S(2)}, u32[]{:S(2)}) %collective-permute-start.3) | collective-permute-done | bytes 16416 | tf_op jit(solution)/shard_map/ppermute | solution.py:39
  59.2 5.9 %collective-permute-done.4 = bf16[64,128]{1,0:T(8,128)(2,1)S(1)} collective-permute-done((bf16[64,128]{1,0:T(8,128)(2,1)S(1)}, bf16[64,128]{1,0:T(8,128)(2,1)S(1)}, u32[]{:S(2)}, u32[]{:S(2)}) %collective-permute-start.4) | collective-permute-done | bytes 16416 | tf_op jit(solution)/shard_map/ppermute | solution.py:39
  65.1 5.9 %collective-permute-done.5 = bf16[64,128]{1,0:T(8,128)(2,1)S(1)} collective-permute-done((bf16[64,128]{1,0:T(8,128)(2,1)S(1)}, bf16[64,128]{1,0:T(8,128)(2,1)S(1)}, u32[]{:S(2)}, u32[]{:S(2)}) %collective-permute-start.5) | collective-permute-done | bytes 16416 | tf_op jit(solution)/shard_map/ppermute | solution.py:39
  70.9 5.9 %collective-permute-done.6 = bf16[64,128]{1,0:T(8,128)(2,1)S(1)} collective-permute-done((bf16[64,128]{1,0:T(8,128)(2,1)S(1)}, bf16[64,128]{1,0:T(8,128)(2,1)S(1)}, u32[]{:S(2)}, u32[]{:S(2)}) %collective-permute-start.6) | collective-permute-done | bytes 16416 | tf_op jit(solution)/shard_map/ppermute | solution.py:39
  76.8 0.1 select_reduce_fusion
  76.9 5.8 %collective-permute-done.7 = bf16[64,128]{1,0:T(8,128)(2,1)S(1)} collective-permute-done((bf16[64,128]{1,0:T(8,128)(2,1)S(1)}, bf16[64,128]{1,0:T(8,128)(2,1)S(1)}, u32[]{:S(2)}, u32[]{:S(2)}) %collective-permute-start.7) | collective-permute-done | bytes 16416 | tf_op jit(solution)/shard_map/ppermute | solution.py:39
  82.7 5.8 %collective-permute-done.8 = bf16[64,128]{1,0:T(8,128)(2,1)S(1)} collective-permute-done((bf16[64,128]{1,0:T(8,128)(2,1)S(1)}, bf16[64,128]{1,0:T(8,128)(2,1)S(1)}, u32[]{:S(2)}, u32[]{:S(2)}) %collective-permute-start.8) | collective-permute-done | bytes 16416 | tf_op jit(solution)/shard_map/ppermute | solution.py:39
  88.5 0.6 fusion.54
  89.1 5.2 %collective-permute-done.9 = bf16[64,128]{1,0:T(8,128)(2,1)S(1)} collective-permute-done((bf16[64,128]{1,0:T(8,128)(2,1)S(1)}, bf16[64,128]{1,0:T(8,128)(2,1)S(1)}, u32[]{:S(2)}, u32[]{:S(2)}) %collective-permute-start.9) | collective-permute-done | bytes 16416 | tf_op jit(solution)/shard_map/ppermute | solution.py:39
  95.0 5.2 %collective-permute-done.10 = bf16[64,128]{1,0:T(8,128)(2,1)S(1)} collective-permute-done((bf16[64,128]{1,0:T(8,128)(2,1)S(1)}, bf16[64,128]{1,0:T(8,128)(2,1)S(1)}, u32[]{:S(2)}, u32[]{:S(2)}) %collective-permute-start.10) | collective-permute-done | bytes 16416 | tf_op jit(solution)/shard_map/ppermute | solution.py:39
  100.2 5.9 %collective-permute-done.11 = bf16[64,128]{1,0:T(8,128)(2,1)S(1)} collective-permute-done((bf16[64,128]{1,0:T(8,128)(2,1)S(1)}, bf16[64,128]{1,0:T(8,128)(2,1)S(1)}, u32[]{:S(2)}, u32[]{:S(2)}) %collective-permute-start.11) | collective-permute-done | bytes 16416 | tf_op jit(solution)/shard_map/ppermute | solution.py:39
  106.1 0.7 copy-done.8
  106.8 0.1 dynamic_slice.37
  106.8 0.1 dynamic_slice.36
  106.9 0.7 copy-done.9
  107.6 0.6 dynamic-slice.3
  108.8 3.2 %collective-permute-done.12 = bf16[64,128]{1,0:T(8,128)(2,1)S(1)} collective-permute-done((bf16[64,128]{1,0:T(8,128)(2,1)S(1)}, bf16[64,128]{1,0:T(8,128)(2,1)S(1)}, u32[]{:S(2)}, u32[]{:S(2)}) %collective-permute-start.12) | collective-permute-done | bytes 16416 | tf_op jit(solution)/shard_map/ppermute | solution.py:39
  112.0 5.9 %collective-permute-done.13 = bf16[64,128]{1,0:T(8,128)(2,1)S(1)} collective-permute-done((bf16[64,128]{1,0:T(8,128)(2,1)S(1)}, bf16[64,128]{1,0:T(8,128)(2,1)S(1)}, u32[]{:S(2)}, u32[]{:S(2)}) %collective-permute-start.13) | collective-permute-done | bytes 16416 | tf_op jit(solution)/shard_map/ppermute | solution.py:39
  117.8 18.3 %all_gather.6 = bf16[512,128]{1,0:T(8,128)(2,1)S(1)} all-gather(bf16[32,128]{1,0:T(8,128)(2,1)S(1)} %constant_dynamic-slice_fusion.1), channel_id=1, replica_groups=mesh['dp'=16,'mp'=2] {'dp'}, dimensions={0}, use_global_device_ids=true | all-gather | bytes 139264 | tf_op jit(solution)/shard_map/all_gather | solution.py:93
  136.6 0.3 fusion.13
  136.9 4.9 %all-reduce.2 = (f32[32]{0:T(128)S(1)}, f32[32]{0:T(128)S(1)}) all-reduce(f32[32]{0:T(128)S(1)} %get-tuple-element.70, f32[32]{0:T(128)S(1)} %get-tuple-element.69), channel_id=1, replica_groups=mesh['dp'=16,'mp'=2] {'mp'}, use_global_device_ids=true, to_apply=%region_6.7 | all-reduce | flops 64 | bytes 512 | tf_op jit(solution)/shard_map/psum | solution.py:71
  141.8 0.2 dynamic-update-slice.1
  142.0 29.5 %all-reduce = f32[512]{0:T(512)S(1)} all-reduce(f32[512]{0:T(512)S(1)} %dynamic-update-slice.1), channel_id=1, replica_groups=mesh['dp'=16,'mp'=2] {'dp'}, use_global_device_ids=true, to_apply=%add | all-reduce | flops 512 | bytes 4096
  171.5 0.2 convolution_dynamic-update-slice_fusion
  171.7 0.3 fusion.10
  172.1 0.6 copy-done.3
  172.8 17.1 %all-reduce.9.cloned.1.call-done = f32[128,128]{1,0:T(8,128)} async-done(((f32[128,128]{1,0:T(8,128)}), f32[128,128]{1,0:T(8,128)}) %all-reduce.9.cloned.1.call-update) | async-done | bytes 65552 | tf_op jit(solution)/shard_map/psum | solution.py:123
  189.9 1.1 multiply_reduce_fusion
  191.0 0.1 divide_convert_fusion
  191.1 0.9 fusion.62
  191.9 0.2 convert_reduce_fusion
  192.1 0.7 copy-done.5
  192.8 1.0 convolution_bitcast_fusion
  193.9 0.5 add_subtract_fusion
  194.4 33.6 %psum.54 = f32[256]{0:T(256)} all-reduce(f32[256]{0:T(256)S(1)} %get-tuple-element.87), channel_id=1, replica_groups=mesh['dp'=16,'mp'=2] {'dp'}, use_global_device_ids=true, to_apply=%region_12.13 | all-reduce | flops 256 | bytes 2048 | tf_op jit(solution)/shard_map/psum | solution.py:136
  228.0 57.8 %all-reduce.11.cloned.1.call-done = (f32[512,256]{0,1:T(8,128)}, f32[256,128]{1,0:T(8,128)}) async-done(((f32[512,256]{0,1:T(8,128)}, f32[256,128]{1,0:T(8,128)}), (f32[512,256]{0,1:T(8,128)}, f32[256,128]{1,0:T(8,128)})) %all-reduce.11.cloned.1.call-update) | async-done | bytes 655376 | tf_op jit(solution)/shard_map/psum | solution.py:136
  285.8 2.1 copy.11
  287.9 0.7 copy.50
  (78 shorter events, 0.6 us)
Async XLA Ops:
  7.2 1.0 copy-start
  7.2 2.1 copy-start.6
  7.2 27.3 %all-reduce.7.cloned.1.call-start = ((), (), s32[]{:S(2)}) async-start(), calls=%async_computation | async-start | bytes 131072 | tf_op jit(solution)/shard_map/psum | solution.py:30
  10.1 179.8 %all-reduce.9.cloned.1.call-start = ((), (), s32[]{:S(2)}) async-start(), calls=%async_computation.1 | async-start | bytes 131072 | tf_op jit(solution)/shard_map/psum | solution.py:123
  34.5 1.0 copy-start.1
  35.7 41.1 %copy-start.7 = (s32[16]{0:T(128)S(1)}, s32[16]{0:T(128)}, u32[]{:S(2)}) copy-start(s32[16]{0:T(128)} %param.11) | copy-start | bytes 196
  35.7 5.9 %collective-permute-start = (bf16[64,128]{1,0:T(8,128)(2,1)S(1)}, bf16[64,128]{1,0:T(8,128)(2,1)S(1)}, u32[]{:S(2)}, u32[]{:S(2)}) collective-permute-start(bf16[64,128]{1,0:T(8,128)(2,1)S(1)} %constant_dynamic-slice_fusion), channel_id=1, source_target_pairs={{0,2},{2,4},{4,6},{6,8},{8,10},{10,12},{12,14},{14,16},{16,18},{18... | collective-permute-start | bytes 49160 | tf_op jit(solution)/shard_map/ppermute | solution.py:39
  41.6 5.9 %collective-permute-start.1 = (bf16[64,128]{1,0:T(8,128)(2,1)S(1)}, bf16[64,128]{1,0:T(8,128)(2,1)S(1)}, u32[]{:S(2)}, u32[]{:S(2)}) collective-permute-start(bf16[64,128]{1,0:T(8,128)(2,1)S(1)} %collective-permute-done), channel_id=1, source_target_pairs={{0,2},{2,4},{4,6},{6,8},{8,10},{10,12},{12,14},{14,16},{16,18},{18... | collective-permute-start | bytes 49160 | tf_op jit(solution)/shard_map/ppermute | solution.py:39
  47.5 5.9 %collective-permute-start.2 = (bf16[64,128]{1,0:T(8,128)(2,1)S(1)}, bf16[64,128]{1,0:T(8,128)(2,1)S(1)}, u32[]{:S(2)}, u32[]{:S(2)}) collective-permute-start(bf16[64,128]{1,0:T(8,128)(2,1)S(1)} %collective-permute-done.1), channel_id=1, source_target_pairs={{0,2},{2,4},{4,6},{6,8},{8,10},{10,12},{12,14},{14,16},{16,18},{18... | collective-permute-start | bytes 49160 | tf_op jit(solution)/shard_map/ppermute | solution.py:39
  53.3 5.9 %collective-permute-start.3 = (bf16[64,128]{1,0:T(8,128)(2,1)S(1)}, bf16[64,128]{1,0:T(8,128)(2,1)S(1)}, u32[]{:S(2)}, u32[]{:S(2)}) collective-permute-start(bf16[64,128]{1,0:T(8,128)(2,1)S(1)} %collective-permute-done.2), channel_id=1, source_target_pairs={{0,2},{2,4},{4,6},{6,8},{8,10},{10,12},{12,14},{14,16},{16,18},{18... | collective-permute-start | bytes 49160 | tf_op jit(solution)/shard_map/ppermute | solution.py:39
  59.2 5.9 %collective-permute-start.4 = (bf16[64,128]{1,0:T(8,128)(2,1)S(1)}, bf16[64,128]{1,0:T(8,128)(2,1)S(1)}, u32[]{:S(2)}, u32[]{:S(2)}) collective-permute-start(bf16[64,128]{1,0:T(8,128)(2,1)S(1)} %collective-permute-done.3), channel_id=1, source_target_pairs={{0,2},{2,4},{4,6},{6,8},{8,10},{10,12},{12,14},{14,16},{16,18},{18... | collective-permute-start | bytes 49160 | tf_op jit(solution)/shard_map/ppermute | solution.py:39
  65.1 5.9 %collective-permute-start.5 = (bf16[64,128]{1,0:T(8,128)(2,1)S(1)}, bf16[64,128]{1,0:T(8,128)(2,1)S(1)}, u32[]{:S(2)}, u32[]{:S(2)}) collective-permute-start(bf16[64,128]{1,0:T(8,128)(2,1)S(1)} %collective-permute-done.4), channel_id=1, source_target_pairs={{0,2},{2,4},{4,6},{6,8},{8,10},{10,12},{12,14},{14,16},{16,18},{18... | collective-permute-start | bytes 49160 | tf_op jit(solution)/shard_map/ppermute | solution.py:39
  70.9 5.9 %collective-permute-start.6 = (bf16[64,128]{1,0:T(8,128)(2,1)S(1)}, bf16[64,128]{1,0:T(8,128)(2,1)S(1)}, u32[]{:S(2)}, u32[]{:S(2)}) collective-permute-start(bf16[64,128]{1,0:T(8,128)(2,1)S(1)} %collective-permute-done.5), channel_id=1, source_target_pairs={{0,2},{2,4},{4,6},{6,8},{8,10},{10,12},{12,14},{14,16},{16,18},{18... | collective-permute-start | bytes 49160 | tf_op jit(solution)/shard_map/ppermute | solution.py:39
  76.8 5.9 %collective-permute-start.7 = (bf16[64,128]{1,0:T(8,128)(2,1)S(1)}, bf16[64,128]{1,0:T(8,128)(2,1)S(1)}, u32[]{:S(2)}, u32[]{:S(2)}) collective-permute-start(bf16[64,128]{1,0:T(8,128)(2,1)S(1)} %collective-permute-done.6), channel_id=1, source_target_pairs={{0,2},{2,4},{4,6},{6,8},{8,10},{10,12},{12,14},{14,16},{16,18},{18... | collective-permute-start | bytes 49160 | tf_op jit(solution)/shard_map/ppermute | solution.py:39
  82.6 5.9 %collective-permute-start.8 = (bf16[64,128]{1,0:T(8,128)(2,1)S(1)}, bf16[64,128]{1,0:T(8,128)(2,1)S(1)}, u32[]{:S(2)}, u32[]{:S(2)}) collective-permute-start(bf16[64,128]{1,0:T(8,128)(2,1)S(1)} %collective-permute-done.7), channel_id=1, source_target_pairs={{0,2},{2,4},{4,6},{6,8},{8,10},{10,12},{12,14},{14,16},{16,18},{18... | collective-permute-start | bytes 49160 | tf_op jit(solution)/shard_map/ppermute | solution.py:39
  88.5 5.9 %collective-permute-start.9 = (bf16[64,128]{1,0:T(8,128)(2,1)S(1)}, bf16[64,128]{1,0:T(8,128)(2,1)S(1)}, u32[]{:S(2)}, u32[]{:S(2)}) collective-permute-start(bf16[64,128]{1,0:T(8,128)(2,1)S(1)} %collective-permute-done.8), channel_id=1, source_target_pairs={{0,2},{2,4},{4,6},{6,8},{8,10},{10,12},{12,14},{14,16},{16,18},{18... | collective-permute-start | bytes 49160 | tf_op jit(solution)/shard_map/ppermute | solution.py:39
  94.4 5.9 %collective-permute-start.10 = (bf16[64,128]{1,0:T(8,128)(2,1)S(1)}, bf16[64,128]{1,0:T(8,128)(2,1)S(1)}, u32[]{:S(2)}, u32[]{:S(2)}) collective-permute-start(bf16[64,128]{1,0:T(8,128)(2,1)S(1)} %collective-permute-done.9), channel_id=1, source_target_pairs={{0,2},{2,4},{4,6},{6,8},{8,10},{10,12},{12,14},{14,16},{16,18},{18... | collective-permute-start | bytes 49160 | tf_op jit(solution)/shard_map/ppermute | solution.py:39
  100.2 5.9 %collective-permute-start.11 = (bf16[64,128]{1,0:T(8,128)(2,1)S(1)}, bf16[64,128]{1,0:T(8,128)(2,1)S(1)}, u32[]{:S(2)}, u32[]{:S(2)}) collective-permute-start(bf16[64,128]{1,0:T(8,128)(2,1)S(1)} %collective-permute-done.10), channel_id=1, source_target_pairs={{0,2},{2,4},{4,6},{6,8},{8,10},{10,12},{12,14},{14,16},{16,18},{18... | collective-permute-start | bytes 49160 | tf_op jit(solution)/shard_map/ppermute | solution.py:39
  106.1 5.9 %collective-permute-start.12 = (bf16[64,128]{1,0:T(8,128)(2,1)S(1)}, bf16[64,128]{1,0:T(8,128)(2,1)S(1)}, u32[]{:S(2)}, u32[]{:S(2)}) collective-permute-start(bf16[64,128]{1,0:T(8,128)(2,1)S(1)} %collective-permute-done.11), channel_id=1, source_target_pairs={{0,2},{2,4},{4,6},{6,8},{8,10},{10,12},{12,14},{14,16},{16,18},{18... | collective-permute-start | bytes 49160 | tf_op jit(solution)/shard_map/ppermute | solution.py:39
  106.1 0.7 copy-start.8
  106.9 0.7 copy-start.9
  112.0 5.9 %collective-permute-start.13 = (bf16[64,128]{1,0:T(8,128)(2,1)S(1)}, bf16[64,128]{1,0:T(8,128)(2,1)S(1)}, u32[]{:S(2)}, u32[]{:S(2)}) collective-permute-start(bf16[64,128]{1,0:T(8,128)(2,1)S(1)} %collective-permute-done.12), channel_id=1, source_target_pairs={{0,2},{2,4},{4,6},{6,8},{8,10},{10,12},{12,14},{14,16},{16,18},{18... | collective-permute-start | bytes 49160 | tf_op jit(solution)/shard_map/ppermute | solution.py:39
  117.8 18.3 %collective-permute-start.14 = (bf16[64,128]{1,0:T(8,128)(2,1)S(1)}, bf16[64,128]{1,0:T(8,128)(2,1)S(1)}, u32[]{:S(2)}, u32[]{:S(2)}) collective-permute-start(bf16[64,128]{1,0:T(8,128)(2,1)S(1)} %collective-permute-done.13), channel_id=1, source_target_pairs={{0,2},{2,4},{4,6},{6,8},{8,10},{10,12},{12,14},{14,16},{16,18},{18... | collective-permute-start | bytes 49160 | tf_op jit(solution)/shard_map/ppermute | solution.py:39
  172.1 0.6 copy-start.3
  172.7 113.1 %all-reduce.11.cloned.1.call-start = ((), (), s32[]{:S(2)}) async-start(), calls=%async_computation.2 | async-start | bytes 1310720 | tf_op jit(solution)/shard_map/psum | solution.py:136
  189.9 1.1 copy-start.2
  191.9 0.9 copy-start.5
  285.8 2.1 copy-start.4
Sparse Core Ops, SparseCore 0:
  10.8 23.6 all-reduce.6
  172.9 16.9 all-reduce.8
  194.0 91.7 all-reduce.10
